TPU v7x, 256 devices: a whole 4x4x8 slice. The times are simulated.
256 devices in a mesh: src: 32 (over x, z_hi, core), freq: 8 (over y, z_lo).
Axes of the slice: x: 4, y: 4, z: 8 (z_hi: 4, z_lo: 2; z = z_hi * 2 + z_lo), core: 2. Of those that a mesh axis runs over, the one named last changes fastest.
Arguments:
- wave: bfloat16 [2, 512, 128, 1024], P(None, 'src', 'freq'), may hold values from -6 to 6
- live: int32 [512], replicated, may hold values from 128 to 1024, as said below
- vel_index: int32 [2, 1536], replicated, may hold values from 0 to 7
- taps: float32 [2, 8, 128, 9], P(None, None, 'freq')
Outputs:
- image: float32 [2, 512, 1024], P(None, 'src')
- wave_out: bfloat16 [2, 512, 128, 1024], P(None, 'src', 'freq')
Inputs may be any that keep to these rules, and one draw needn't show every extreme that they name: `live`: shot 0 has all 1024 columns and shot 1 has 128.
All inputs are finite; a program needn't handle non-finite values.
Results may differ from a plain program's by a relative error of at most 0.0064.
Values may be sent and summed in bfloat16 or wider, within the bound.
A program may use at most 192 MiB of HBM per device.

v0:
```python
import functools

import jax
import jax.numpy as jnp
from jax import lax
from jax.experimental import pallas as pl
from jax.experimental.pallas import tpu as pltpu
from jax.sharding import PartitionSpec as P

MESH = pl.DeviceIdType.MESH
LANES = 128
F32 = jnp.float32
BF16 = jnp.bfloat16


def lane_iota(rows=8):
    return lax.broadcasted_iota(jnp.int32, (rows, LANES), 1)


def shifted(load, block, blocks, delta, lane):
    here = load(block)
    if isinstance(delta, int) and delta == 0:
        return here
    if delta > 0:
        other = load(block + 1) if block + 1 < blocks else jnp.zeros_like(here)
        return pltpu.roll(jnp.where(lane < delta, other, here), LANES - delta, 1)
    other = load(block - 1) if block > 0 else jnp.zeros_like(here)
    return pltpu.roll(jnp.where(lane >= LANES + delta, other, here), -delta, 1)


def keep_mask(lane, block, shot, live):
    h = lane + (LANES * block - shot)
    return (h >= 0) & (h < live)


def load_skewed(wave_ref, x_ref, shot, live, blocks):
    data = wave_ref.shape[-1] // LANES
    lane = lane_iota(16)
    for c in range(2):
        prev = jnp.zeros((16, LANES), F32)
        for b in range(blocks):
            if b < data:
                here = wave_ref[c, shot, :, b * LANES : (b + 1) * LANES].astype(F32)
            else:
                here = jnp.zeros((16, LANES), F32)
            moved = pltpu.roll(jnp.where(lane >= LANES - shot, prev, here), shot, 1)
            keep = keep_mask(lane, b, shot, live)
            x_ref[shot, c, :, b * LANES : (b + 1) * LANES] = jnp.where(keep, moved, 0.0)
            prev = here


def receiver_row(x_ref, coef_ref, depth, r_ref, shot, row, live, blocks):
    lane = lane_iota()
    taps = coef_ref.shape[1]
    half = (taps - 1) // 2
    for b in range(blocks):
        cols = slice(b * LANES, (b + 1) * LANES)
        keep = keep_mask(lane, b, shot, live)
        parts = [[], []]
        for part in range(2):
            rows = slice(part * 8, part * 8 + 8)

            def load(c):
                return lambda i: x_ref[shot, c, rows, i * LANES : (i + 1) * LANES]

            acc_re = acc_im = None
            for k in range(taps):
                x_re = shifted(load(0), b, blocks, k - half, lane)
                x_im = shifted(load(1), b, blocks, k - half, lane)
                c_re = coef_ref[depth, k, 0, rows, cols]
                c_im = coef_ref[depth, k, 1, rows, cols]
                re = c_re * x_re - c_im * x_im
                im = c_re * x_im + c_im * x_re
                acc_re = re if acc_re is None else acc_re + re
                acc_im = im if acc_im is None else acc_im + im
            parts[0].append(jnp.where(keep, acc_re, 0.0))
            parts[1].append(jnp.where(keep, acc_im, 0.0))
        for c in range(2):
            r_ref[row, c, :, cols] = jnp.concatenate(parts[c], axis=0).astype(BF16)


def build_coef(table_ref, vseg_ref, coef_ref, depth, blocks):
    taps = coef_ref.shape[1]
    level = lax.broadcasted_iota(jnp.int32, (24, LANES), 0) % 8
    for b in range(blocks):
        cols = slice(b * LANES, (b + 1) * LANES)
        onehot = (vseg_ref[depth : depth + 1, cols] == level).astype(F32).astype(BF16)
        out = jnp.dot(table_ref[...], onehot, preferred_element_type=F32)
        coef_ref[depth, :, :, :, cols] = out.reshape(taps, 2, 16, LANES)


def build_weights(expand_ref, vshot_ref, w_ref, depth, half):
    width = expand_ref.shape[2]
    for s in range(8):
        block = expand_ref[vshot_ref[depth, half * 8 + s]]
        lead, rest = divmod(32 * s, LANES)
        if rest:
            block = pltpu.roll(block, rest, 1)
        block = block.astype(BF16)
        rows = slice(s * 32, s * 32 + 32)
        w_ref[half, rows, :] = jnp.zeros((32, 512), BF16)
        fit = min(width, 512 - lead * LANES)
        w_ref[half, rows, lead * LANES : lead * LANES + fit] = block[:, :fit]


def place_halo(halo_ref, r_ref, row, delta, blocks):
    lane = lane_iota(16)
    for i in range(4):
        for c in range(2):
            load = lambda j: halo_ref[i, c, :, j * LANES : (j + 1) * LANES].astype(F32)
            for b in range(blocks):
                moved = shifted(load, b, blocks, delta, lane)
                r_ref[row + i, c, :, b * LANES : (b + 1) * LANES] = moved.astype(BF16)


def shot_step(w_ref, r_ref, x_ref, live_ref, half, lo, hi):
    lane = lane_iota(16)
    cols = slice(lo * LANES, hi * LANES)
    rhs = r_ref[half * 8 : half * 8 + 16, :, :, cols].reshape(512, (hi - lo) * LANES)
    y = jnp.dot(w_ref[half], rhs, preferred_element_type=F32)
    for s in range(8):
        shot = half * 8 + s
        for b in range(lo, hi):
            keep = keep_mask(lane, b, shot, live_ref[shot])
            for c in range(2):
                part = y[s * 32 + c * 16 : s * 32 + c * 16 + 16, (b - lo) * LANES : (b - lo + 1) * LANES]
                part = part.astype(BF16).astype(F32)
                x_ref[shot, c, :, b * LANES : (b + 1) * LANES] = jnp.where(keep, part, 0.0)


def unskew(load, block, blocks, shot, lane):
    here = load(block)
    if isinstance(shot, int) and shot == 0:
        return here
    other = load(block + 1)
    return pltpu.roll(jnp.where(lane < shot, other, here), LANES - shot, 1)


def put_image(x_ref, image_ref, data):
    for shot in range(x_ref.shape[0]):
        sums = [jnp.sum(x_ref[shot, 0, :, b * LANES : (b + 1) * LANES], axis=0, keepdims=True) for b in range(data + 1)]
        for b in range(data):
            moved = unskew(lambda i: jnp.broadcast_to(sums[i], (8, LANES)), b, data + 1, shot, lane_iota())
            image_ref[shot : shot + 1, b * LANES : (b + 1) * LANES] = moved[:1]


def first_kernel(live_ref, wave_ref, vseg_ref, table_ref, r_ref, x_ref, coef_ref):
    blocks = r_ref.shape[-1] // LANES
    build_coef(table_ref, vseg_ref, coef_ref, 0, blocks)

    def body(shot, carry):
        load_skewed(wave_ref, x_ref, shot, live_ref[shot], blocks)
        receiver_row(x_ref, coef_ref, 0, r_ref, shot, shot, live_ref[shot], blocks)
        return carry

    lax.fori_loop(0, 16, body, 0)


def middle_kernel(live_ref, vshot_ref, vseg_ref, table_ref, expand_ref, r_in_ref, before_ref, after_ref,
                  r_ref, image_ref, x_ref, coef_ref, w_ref, wide_ref):
    blocks = r_ref.shape[-1] // LANES
    data = image_ref.shape[-1] // LANES
    build_coef(table_ref, vseg_ref, coef_ref, 0, blocks)
    for half in range(2):
        build_weights(expand_ref, vshot_ref, w_ref, 0, half)
    wide_ref[4:20] = r_in_ref[...]
    place_halo(before_ref, wide_ref, 0, 16, blocks)
    place_halo(after_ref, wide_ref, 20, -16, blocks)
    for half in range(2):
        for lo in range(0, blocks, 3):
            shot_step(w_ref, wide_ref, x_ref, live_ref, half, lo, lo + 3)

    put_image(x_ref, image_ref, data)

    def body(shot, carry):
        receiver_row(x_ref, coef_ref, 0, r_ref, shot, shot, live_ref[shot], blocks)
        return carry

    lax.fori_loop(0, 16, body, 0)


def last_kernel(live_ref, vshot_ref, expand_ref, r_in_ref, before_ref, after_ref,
                out_ref, image_ref, x_ref, w_ref, wide_ref):
    blocks = wide_ref.shape[-1] // LANES
    data = image_ref.shape[-1] // LANES
    for half in range(2):
        build_weights(expand_ref, vshot_ref, w_ref, 0, half)
    wide_ref[4:20] = r_in_ref[...]
    place_halo(before_ref, wide_ref, 0, 16, blocks)
    place_halo(after_ref, wide_ref, 20, -16, blocks)
    for half in range(2):
        for lo in range(0, blocks, 3):
            shot_step(w_ref, wide_ref, x_ref, live_ref, half, lo, lo + 3)

    put_image(x_ref, image_ref, data)
    lane = lane_iota(16)

    def body(shot, carry):
        for c in range(2):
            load = lambda i: x_ref[shot, c, :, i * LANES : (i + 1) * LANES]
            for b in range(data):
                out_ref[c, shot, :, b * LANES : (b + 1) * LANES] = unskew(load, b, blocks, shot, lane).astype(BF16)
        return carry

    lax.fori_loop(0, 16, body, 0)


def reduce_kernel(peers, first_ref, second_ref, out_ref, parts, got, total, full, sems):
    me = lax.axis_index("freq")
    rows = first_ref.shape[0]
    barrier = pltpu.get_barrier_semaphore()
    for step in range(1, peers):
        pl.semaphore_signal(barrier, inc=1, device_id={"freq": lax.rem(me + step, peers)}, device_id_type=MESH)
    for q in range(peers):
        parts[q, 0:rows, :] = first_ref[:, q * LANES : (q + 1) * LANES]
        parts[q, rows : 2 * rows, :] = second_ref[:, q * LANES : (q + 1) * LANES]
    pl.semaphore_wait(barrier, peers - 1)

    def scatter(step):
        peer = lax.rem(me + step, peers)
        return pltpu.make_async_remote_copy(
            src_ref=parts.at[peer], dst_ref=got.at[step], send_sem=sems.at[0, step], recv_sem=sems.at[1, step],
            device_id={"freq": peer}, device_id_type=MESH)

    def gather(step):
        peer = lax.rem(me + step, peers)
        return pltpu.make_async_remote_copy(
            src_ref=total, dst_ref=full.at[step], send_sem=sems.at[2, step], recv_sem=sems.at[3, step],
            device_id={"freq": peer}, device_id_type=MESH)

    for step in range(1, peers):
        scatter(step).start()
    value = parts[me]
    for step in range(1, peers):
        scatter(step).wait()
        value = value + got[step]
    total[...] = value
    for step in range(1, peers):
        gather(step).start()
    cols = pl.ds(pl.multiple_of(me * LANES, LANES), LANES)
    out_ref[0, :, cols] = value[:rows]
    out_ref[1, :, cols] = value[rows:]
    for step in range(1, peers):
        gather(step).wait()
        owner = lax.rem(me + peers - step, peers)
        cols = pl.ds(pl.multiple_of(owner * LANES, LANES), LANES)
        out_ref[0, :, cols] = full[step, 0:rows, :]
        out_ref[1, :, cols] = full[step, rows : 2 * rows, :]


def split3(value):
    high = lax.reduce_precision(value, 8, 7)
    rest = value - high
    mid = lax.reduce_precision(rest, 8, 7)
    low = rest - mid
    return jnp.concatenate([high, mid, low], axis=-1).astype(BF16)


def tap_tables(taps):
    _, levels, freqs, count = taps.shape
    table = split3(jnp.transpose(taps, (3, 0, 2, 1)).reshape(count * 2 * freqs, levels))
    re, im = taps[0], taps[1]
    mix = jnp.stack([jnp.stack([re, -im], -1), jnp.stack([im, re], -1)], 1)
    same = jnp.eye(freqs, dtype=F32)
    expand = mix[..., None] * same[None, None, :, None, None, :]
    expand = expand.reshape(levels, 2 * freqs, count * 2 * freqs)
    return table, jnp.pad(expand, ((0, 0), (0, 0), (0, 384 - expand.shape[2])))


def local(wave, live, vel_index, taps):
    shots, freqs, width = wave.shape[1:]
    wide = width + LANES
    n_src = lax.axis_size("src")
    n_freq = lax.axis_size("freq")
    first = lax.axis_index("src") * shots
    live_here = lax.dynamic_slice_in_dim(live, first, shots)
    vshot = lax.dynamic_slice_in_dim(vel_index, first, shots, axis=1)
    vseg = lax.dynamic_slice_in_dim(jnp.pad(vel_index, ((0, 0), (0, LANES))), first, wide, axis=1)
    table, expand = tap_tables(taps)

    smem = pl.BlockSpec(memory_space=pltpu.SMEM)
    vmem = pl.BlockSpec(memory_space=pltpu.VMEM)
    x_buf = pltpu.VMEM((shots, 2, freqs, wide), F32)
    coef_buf = pltpu.VMEM((1, taps.shape[3], 2, freqs, wide), F32)
    w_buf = pltpu.VMEM((2, 256, 512), BF16)
    wide_buf = pltpu.VMEM((shots + 8, 2, freqs, wide), BF16)
    r_shape = jax.ShapeDtypeStruct((shots, 2, freqs, wide), BF16)
    image_shape = jax.ShapeDtypeStruct((shots, width), F32)
    up = [(i, i + 1) for i in range(n_src - 1)]
    down = [(i + 1, i) for i in range(n_src - 1)]

    r = pl.pallas_call(
        first_kernel, out_shape=r_shape, in_specs=[smem, vmem, vmem, vmem], out_specs=vmem,
        scratch_shapes=[x_buf, coef_buf],
    )(live_here, wave, vseg[0:1], table)
    before = lax.ppermute(r[shots - 4 :], "src", up)
    after = lax.ppermute(r[:4], "src", down)
    r, image0 = pl.pallas_call(
        middle_kernel, out_shape=(r_shape, image_shape),
        in_specs=[smem, smem] + [vmem] * 6, out_specs=(vmem, vmem),
        scratch_shapes=[x_buf, coef_buf, w_buf, wide_buf],
    )(live_here, vshot[0:1], vseg[1:2], table, expand, r, before, after)
    before = lax.ppermute(r[shots - 4 :], "src", up)
    after = lax.ppermute(r[:4], "src", down)
    wave_out, image1 = pl.pallas_call(
        last_kernel, out_shape=(jax.ShapeDtypeStruct(wave.shape, BF16), image_shape),
        in_specs=[smem, smem] + [vmem] * 4, out_specs=(vmem, vmem),
        scratch_shapes=[x_buf, w_buf, wide_buf],
    )(live_here, vshot[1:2], expand, r, before, after)
    piece = pltpu.VMEM((n_freq, 2 * shots, LANES), F32)
    image = pl.pallas_call(
        functools.partial(reduce_kernel, n_freq),
        out_shape=jax.ShapeDtypeStruct((2, shots, width), F32),
        in_specs=[vmem, vmem], out_specs=vmem,
        scratch_shapes=[piece, piece, pltpu.VMEM((2 * shots, LANES), F32), piece, pltpu.SemaphoreType.DMA((4, n_freq))],
        compiler_params=pltpu.CompilerParams(collective_id=0, has_side_effects=True),
    )(image0, image1)
    return image, wave_out


def solution(mesh):
    placed = (P(None, "src", "freq", None), P(), P(), P(None, None, "freq", None))
    return jax.shard_map(
        local, mesh=mesh, in_specs=placed,
        out_specs=(P(None, "src", None), P(None, "src", "freq", None)), check_vma=False,
    )
```

profile of v0, /device:TPU:6, one launch (start us, length us, event | category | flops | bytes accessed | tf_op | source)
XLA Modules:
  0.0 87.1 jit_solution(2278017630900874201)
XLA Ops:
  0.6 0.9 %copy.8 = f32[9,2,16,8]{2,1,0,3:T(2,128)S(1)} copy(f32[9,2,16,8]{2,3,0,1:T(8,128)} %bitcast.13) | data formatting | bytes 18432 | tf_op jit(solution)/shard_map/transpose | solution.py:261
  1.6 0.1 reshape.29
  1.7 0.7 copy.11.table_ref
  2.4 1.2 %dynamic_slice.9.live_ref = s32[16]{0:T(128)} dynamic-slice(s32[512]{0:T(512)} %param.5, s32[]{:T(128)S(6)} %select_n.9), dynamic_slice_sizes={16} | dynamic-slice | bytes 132 | tf_op jit(solution)/shard_map/dynamic_slice | solution.py:276
  3.7 1.5 %pad_dynamic-slice_fusion.1 = (s32[1,1152]{1,0:T(1,128)}, s32[1,1152]{1,0:T(1,128)}) fusion(s32[]{:T(128)S(6)} %select_n.11, s32[2,1536]{1,0:T(2,128)} %param.6, s32[]{:T(128)S(6)} %add.16), kind=kLoop, calls=%fused_computation.13 | loop fusion | bytes 21512 | tf_op jit(solution)/shard_map/slice | solution.py:295
  5.1 9.3 %shard_map.59.r_in_ref = bf16[16,2,16,1152]{3,2,1,0:T(8,128)(2,1)} custom-call(s32[16]{0:T(128)} %dynamic_slice.9.live_ref, bf16[2,16,16,1024]{3,2,1,0:T(8,128)(2,1)} %wave_ref.1, s32[1,1152]{1,0:T(1,128)} %get-tuple-element.18.vseg_ref, bf16[288,24]{1,0:T(8,128)(2,1)} %copy.11.table_ref), custom_call_target="tpu_custom_call" | custom-call | tf_op jit(solution)/shard_map/pallas_call | solution.py:292
  14.4 1.9 %fusion.4 = (bf16[4,2,16,1152]{3,2,1,0:T(8,128)(2,1)}, bf16[4,2,16,1152]{3,2,1,0:T(8,128)(2,1)}) fusion(bf16[16,2,16,1152]{3,2,1,0:T(8,128)(2,1)} %shard_map.59.r_in_ref), kind=kLoop, calls=%fused_computation.19 | loop fusion | bytes 1179648 | tf_op jit(solution)/shard_map/slice | solution.py:297
  16.3 1.9 %collective-permute-start = (bf16[4,2,16,1152]{3,2,1,0:T(8,128)(2,1)}, bf16[4,2,16,1152]{3,2,1,0:T(8,128)(2,1)S(1)}, u32[]{:S(2)}, u32[]{:S(2)}) collective-permute-start(bf16[4,2,16,1152]{3,2,1,0:T(8,128)(2,1)} %get-tuple-element.13), channel_id=1, source_target_pairs={{0,8},{8,16},{16,24},{24,32},{32,40},{40,48},{48,56},{56,64},{64,7... | collective-permute-start | bytes 884744 | tf_op jit(solution)/shard_map/ppermute | solution.py:296
  18.2 7.9 %collective-permute-start.1 = (bf16[4,2,16,1152]{3,2,1,0:T(8,128)(2,1)}, bf16[4,2,16,1152]{3,2,1,0:T(8,128)(2,1)S(1)}, u32[]{:S(2)}, u32[]{:S(2)}) collective-permute-start(bf16[4,2,16,1152]{3,2,1,0:T(8,128)(2,1)} %get-tuple-element.12), channel_id=1, source_target_pairs={{8,0},{16,8},{24,16},{32,24},{40,32},{48,40},{56,48},{64,56},{72,6... | collective-permute-start | bytes 884744 | tf_op jit(solution)/shard_map/ppermute | solution.py:297
  26.2 2.3 %copy.9 = f32[8,2,16,9,2]{4,3,2,1,0:T(8,128)} copy(f32[8,2,16,9,2]{2,0,3,4,1:T(8,128)S(1)} %pad_maximum_fusion) | data formatting | bytes 36864 | tf_op jit(solution)/shard_map/stack | solution.py:263
  28.6 4.9 %mul.24 = f32[8,2,16,9,2,16]{5,4,3,2,1,0:T(2,128)S(1)} broadcast(f32[8,2,16,9,2]{4,3,2,1,0:T(8,128)} %copy.9), dimensions={0,1,2,3,4} | broadcast | bytes 313344 | tf_op jit(solution)/shard_map/mul | solution.py:265
  33.5 1.6 %mul.25 = f32[8,32,288]{2,1,0:T(8,128)S(1)} reshape(f32[8,2,16,9,2,16]{5,4,3,2,1,0:T(2,128)S(1)} %mul.24) | data formatting | bytes 589824 | tf_op jit(solution)/shard_map/mul | solution.py:265
  35.1 0.1 mul.26
  35.2 0.2 mul.27
  35.4 0.8 pad.9.expand_ref
  36.2 0.7 constant_dynamic-slice_fusion
  37.0 0.6 fusion.5
  37.6 0.0 collective-permute-done.before_ref
  37.6 0.0 collective-permute-done.1.after_ref
  37.6 0.0 copy-start.2
  37.6 0.7 copy-done.1
  38.3 0.1 copy-done.2
  38.4 10.0 %shard_map.60 = (bf16[16,2,16,1152]{3,2,1,0:T(8,128)(2,1)}, f32[16,1024]{1,0:T(8,128)}) custom-call(s32[16]{0:T(128)} %dynamic_slice.9.live_ref, s32[1,16]{1,0:T(1,128)} %get-tuple-element.24.vshot_ref, s32[1,1152]{1,0:T(1,128)} %get-tuple-element.19.vseg_ref, bf16[288,24]{1,0:T(8,128)(2,1)} %copy.11.table_ref, f32[8,32,384]{2,1,0:T(8,128)} %pad.9.expand_ref, ...), custom_call_target="tpu_custom_call" | custom-call | tf_op jit(solution)/shard_map/pallas_call | solution.py:298
  48.3 1.1 %fusion.3 = (bf16[4,2,16,1152]{3,2,1,0:T(8,128)(2,1)S(1)}, bf16[4,2,16,1152]{3,2,1,0:T(8,128)(2,1)S(1)}) fusion(bf16[16,2,16,1152]{3,2,1,0:T(8,128)(2,1)} %get-tuple-element.7.r_in_ref), kind=kLoop, calls=%fused_computation.18 | loop fusion | bytes 1179648 | tf_op jit(solution)/shard_map/slice | solution.py:304
  49.4 1.9 %collective-permute-start.2 = (bf16[4,2,16,1152]{3,2,1,0:T(8,128)(2,1)S(1)}, bf16[4,2,16,1152]{3,2,1,0:T(8,128)(2,1)S(1)}, u32[]{:S(2)}, u32[]{:S(2)}) collective-permute-start(bf16[4,2,16,1152]{3,2,1,0:T(8,128)(2,1)S(1)} %get-tuple-element.11), channel_id=1, source_target_pairs={{0,8},{8,16},{16,24},{24,32},{32,40},{40,48},{48,56},{56,64},{64,7... | collective-permute-start | bytes 884744 | tf_op jit(solution)/shard_map/ppermute | solution.py:303
  51.4 6.7 %collective-permute-start.3 = (bf16[4,2,16,1152]{3,2,1,0:T(8,128)(2,1)S(1)}, bf16[4,2,16,1152]{3,2,1,0:T(8,128)(2,1)S(1)}, u32[]{:S(2)}, u32[]{:S(2)}) collective-permute-start(bf16[4,2,16,1152]{3,2,1,0:T(8,128)(2,1)S(1)} %get-tuple-element.10), channel_id=1, source_target_pairs={{8,0},{16,8},{24,16},{32,24},{40,32},{48,40},{56,48},{64,56},{72,6... | collective-permute-start | bytes 884744 | tf_op jit(solution)/shard_map/ppermute | solution.py:304
  58.0 5.6 %collective-permute-done.2.before_ref = bf16[4,2,16,1152]{3,2,1,0:T(8,128)(2,1)S(1)} collective-permute-done((bf16[4,2,16,1152]{3,2,1,0:T(8,128)(2,1)S(1)}, bf16[4,2,16,1152]{3,2,1,0:T(8,128)(2,1)S(1)}, u32[]{:S(2)}, u32[]{:S(2)}) %collective-permute-start.2) | collective-permute-done | bytes 294944 | tf_op jit(solution)/shard_map/ppermute | solution.py:303
  63.7 1.8 %collective-permute-done.3.after_ref = bf16[4,2,16,1152]{3,2,1,0:T(8,128)(2,1)S(1)} collective-permute-done((bf16[4,2,16,1152]{3,2,1,0:T(8,128)(2,1)S(1)}, bf16[4,2,16,1152]{3,2,1,0:T(8,128)(2,1)S(1)}, u32[]{:S(2)}, u32[]{:S(2)}) %collective-permute-start.3) | collective-permute-done | bytes 294944 | tf_op jit(solution)/shard_map/ppermute | solution.py:304
  65.5 0.7 copy-done.4
  66.2 5.1 %shard_map.61 = (bf16[2,16,16,1024]{3,2,1,0:T(8,128)(2,1)}, f32[16,1024]{1,0:T(8,128)}) custom-call(s32[16]{0:T(128)} %dynamic_slice.9.live_ref, s32[1,16]{1,0:T(1,128)} %get-tuple-element.23.vshot_ref, f32[8,32,384]{2,1,0:T(8,128)} %pad.9.expand_ref, bf16[16,2,16,1152]{3,2,1,0:T(8,128)(2,1)} %get-tuple-element.7.r_in_ref, ...), custom_call_target="tpu_custom_call" | custom-call | tf_op jit(solution)/shard_map/pallas_call | solution.py:305
  71.3 14.3 %shard_map.62 = f32[2,16,1024]{2,1,0:T(8,128)} custom-call(f32[16,1024]{1,0:T(8,128)} %get-tuple-element.6.first_ref, f32[16,1024]{1,0:T(8,128)} %get-tuple-element.8.second_ref), custom_call_target="tpu_custom_call" | custom-call | tf_op jit(solution)/shard_map/pallas_call | solution.py:311
  85.6 1.6 %copy.13 = f32[2,16,1024]{2,1,0:T(8,128)} copy(f32[2,16,1024]{2,1,0:T(8,128)} %shard_map.62) | data formatting | bytes 262144
  (14 shorter events, 0.1 us)
Async XLA Ops:
  5.1 21.0 %copy-start = (f32[2,8,16,9]{2,1,3,0:T(8,128)S(1)}, f32[2,8,16,9]{2,1,3,0:T(8,128)}, u32[]{:S(2)}) copy-start(f32[2,8,16,9]{2,1,3,0:T(8,128)} %param.7) | copy-start | bytes 27652
  16.3 21.2 %collective-permute-start = (bf16[4,2,16,1152]{3,2,1,0:T(8,128)(2,1)}, bf16[4,2,16,1152]{3,2,1,0:T(8,128)(2,1)S(1)}, u32[]{:S(2)}, u32[]{:S(2)}) collective-permute-start(bf16[4,2,16,1152]{3,2,1,0:T(8,128)(2,1)} %get-tuple-element.13), channel_id=1, source_target_pairs={{0,8},{8,16},{16,24},{24,32},{32,40},{40,48},{48,56},{56,64},{64,7... | collective-permute-start | bytes 884744 | tf_op jit(solution)/shard_map/ppermute | solution.py:296
  18.2 19.3 %collective-permute-start.1 = (bf16[4,2,16,1152]{3,2,1,0:T(8,128)(2,1)}, bf16[4,2,16,1152]{3,2,1,0:T(8,128)(2,1)S(1)}, u32[]{:S(2)}, u32[]{:S(2)}) collective-permute-start(bf16[4,2,16,1152]{3,2,1,0:T(8,128)(2,1)} %get-tuple-element.12), channel_id=1, source_target_pairs={{8,0},{16,8},{24,16},{32,24},{40,32},{48,40},{56,48},{64,56},{72,6... | collective-permute-start | bytes 884744 | tf_op jit(solution)/shard_map/ppermute | solution.py:297
  37.6 0.7 copy-start.1
  37.6 0.8 copy-start.2
  49.4 14.2 %collective-permute-start.2 = (bf16[4,2,16,1152]{3,2,1,0:T(8,128)(2,1)S(1)}, bf16[4,2,16,1152]{3,2,1,0:T(8,128)(2,1)S(1)}, u32[]{:S(2)}, u32[]{:S(2)}) collective-permute-start(bf16[4,2,16,1152]{3,2,1,0:T(8,128)(2,1)S(1)} %get-tuple-element.11), channel_id=1, source_target_pairs={{0,8},{8,16},{16,24},{24,32},{32,40},{40,48},{48,56},{56,64},{64,7... | collective-permute-start | bytes 884744 | tf_op jit(solution)/shard_map/ppermute | solution.py:303
  51.4 14.1 %collective-permute-start.3 = (bf16[4,2,16,1152]{3,2,1,0:T(8,128)(2,1)S(1)}, bf16[4,2,16,1152]{3,2,1,0:T(8,128)(2,1)S(1)}, u32[]{:S(2)}, u32[]{:S(2)}) collective-permute-start(bf16[4,2,16,1152]{3,2,1,0:T(8,128)(2,1)S(1)} %get-tuple-element.10), channel_id=1, source_target_pairs={{8,0},{16,8},{24,16},{32,24},{40,32},{48,40},{56,48},{64,56},{72,6... | collective-permute-start | bytes 884744 | tf_op jit(solution)/shard_map/ppermute | solution.py:304
  63.7 1.8 %copy-start.3 = (bf16[4,2,16,1152]{3,2,1,0:T(8,128)(2,1)}, bf16[4,2,16,1152]{3,2,1,0:T(8,128)(2,1)S(1)}, u32[]{:S(2)}) copy-start(bf16[4,2,16,1152]{3,2,1,0:T(8,128)(2,1)S(1)} %collective-permute-done.2.before_ref) | copy-start | bytes 884740
  65.4 0.7 copy-start.4
where the time goes:
time: 87.7 us; the launch traced here: 87.1 us
  Pallas kernels  38.6 us (44%)
  local copies, waits for them, and re-layouts  21.8 us (25%)
  starting transfers between devices  18.4 us (21%)
  waiting for transfers between devices  7.42 us (8%)
    ppermute x2, starting transfers between devices, local(): after = lax.ppermute(r[:4], 'src', down)  14.6 us
    pallas_call x1, Pallas kernels, local(): pl.pallas_call(functools.partial(reduce_kernel, n_freq), out_shape=jax.Sh...  14.3 us
    pallas_call x1, Pallas kernels, local(): pl.pallas_call(middle_kernel, out_shape=(r_shape, image_shape), in_specs=...  9.98 us
    pallas_call x1, Pallas kernels, local(): pl.pallas_call(first_kernel, out_shape=r_shape, in_specs=[smem, vmem, vme...  9.26 us
    mul x4, local copies, waits for them, and re-layouts, tap_tables(): expand = mix[..., None] * same[None, None, :, None, None, :]  6.82 us
    ppermute x2, waiting for transfers between devices, local(): before = lax.ppermute(r[shots - 4:], 'src', up)  5.63 us
    pallas_call x1, Pallas kernels, local(): pl.pallas_call(last_kernel, out_shape=(jax.ShapeDtypeStruct(wave.shape, B...  5.12 us
    ppermute x2, starting transfers between devices, local(): before = lax.ppermute(r[shots - 4:], 'src', up)  3.83 us
  transfers between devices with their start and end apart: 4, of which 2 were waited for; matrix products, arithmetic and copies ran while one was open for 13% of the time, Pallas kernels for 0%

commit v1 on v0

v1 whole, which is shorter than its diff:
```python
import functools

import jax
import jax.numpy as jnp
from jax import lax
from jax.experimental import pallas as pl
from jax.experimental.pallas import tpu as pltpu
from jax.sharding import PartitionSpec as P

MESH = pl.DeviceIdType.MESH
LANES = 128
F32 = jnp.float32
BF16 = jnp.bfloat16


def lane_iota(rows=8):
    return lax.broadcasted_iota(jnp.int32, (rows, LANES), 1)


def shifted(load, block, blocks, delta, lane):
    here = load(block)
    if isinstance(delta, int) and delta == 0:
        return here
    if delta > 0:
        other = load(block + 1) if block + 1 < blocks else jnp.zeros_like(here)
        return pltpu.roll(jnp.where(lane < delta, other, here), LANES - delta, 1)
    other = load(block - 1) if block > 0 else jnp.zeros_like(here)
    return pltpu.roll(jnp.where(lane >= LANES + delta, other, here), -delta, 1)


def keep_mask(lane, block, shot, live):
    h = lane + (LANES * block - shot)
    return (h >= 0) & (h < live)


def load_skewed(wave_ref, x_ref, shot, live, blocks):
    data = wave_ref.shape[-1] // LANES
    lane = lane_iota(16)
    for c in range(2):
        prev = jnp.zeros((16, LANES), F32)
        for b in range(blocks):
            if b < data:
                here = wave_ref[c, shot, :, b * LANES : (b + 1) * LANES].astype(F32)
            else:
                here = jnp.zeros((16, LANES), F32)
            moved = pltpu.roll(jnp.where(lane >= LANES - shot, prev, here), shot, 1)
            keep = keep_mask(lane, b, shot, live)
            x_ref[shot, c, :, b * LANES : (b + 1) * LANES] = jnp.where(keep, moved, 0.0)
            prev = here


def receiver_row(x_ref, coef_ref, depth, r_ref, shot, row, live, blocks):
    lane = lane_iota()
    taps = coef_ref.shape[1]
    half = (taps - 1) // 2
    for b in range(blocks):
        cols = slice(b * LANES, (b + 1) * LANES)
        keep = keep_mask(lane, b, shot, live)
        parts = [[], []]
        for part in range(2):
            rows = slice(part * 8, part * 8 + 8)

            def load(c):
                return lambda i: x_ref[shot, c, rows, i * LANES : (i + 1) * LANES]

            acc_re = acc_im = None
            for k in range(taps):
                x_re = shifted(load(0), b, blocks, k - half, lane)
                x_im = shifted(load(1), b, blocks, k - half, lane)
                c_re = coef_ref[depth, k, 0, rows, cols]
                c_im = coef_ref[depth, k, 1, rows, cols]
                re = c_re * x_re - c_im * x_im
                im = c_re * x_im + c_im * x_re
                acc_re = re if acc_re is None else acc_re + re
                acc_im = im if acc_im is None else acc_im + im
            parts[0].append(jnp.where(keep, acc_re, 0.0))
            parts[1].append(jnp.where(keep, acc_im, 0.0))
        for c in range(2):
            r_ref[depth, row, c, :, cols] = jnp.concatenate(parts[c], axis=0).astype(BF16)


def build_tables(taps_ref, row_ref, swap_ref, table_ref, expand_ref):
    _, count, levels, freqs = taps_ref.shape
    row_ref[...] = jnp.zeros_like(row_ref)
    swap_ref[...] = jnp.zeros_like(swap_ref)
    for k in range(count):
        for c in range(2):
            piece = taps_ref[c, k]
            at = (2 * k + c) * freqs
            row_ref[:, at : at + freqs] = piece
            at = (2 * k + 1 - c) * freqs
            swap_ref[:, at : at + freqs] = piece
    row = row_ref[...]
    swap = swap_ref[...]
    high = row.astype(BF16)
    rest = row - high.astype(F32)
    mid = rest.astype(BF16)
    low = (rest - mid.astype(F32)).astype(BF16)
    table_ref[...] = jnp.concatenate([high.astype(F32), mid.astype(F32), low.astype(F32)], axis=0).astype(BF16)
    lane = lax.broadcasted_iota(jnp.int32, row.shape, 1)
    real = jnp.where((lane // freqs) % 2 == 1, -row, row)
    lane = lax.broadcasted_iota(jnp.int32, (freqs, row.shape[1]), 1)
    same = lane % freqs == lax.broadcasted_iota(jnp.int32, (freqs, row.shape[1]), 0)
    for v in range(levels):
        for c, source in enumerate((real, swap)):
            line = jnp.broadcast_to(source[v : v + 1], same.shape)
            expand_ref[v, c * freqs : (c + 1) * freqs, :] = jnp.where(same, line, 0.0)


def build_coef(table_ref, vel_ref, coef_ref, depth, first, blocks):
    taps = coef_ref.shape[1]
    level = lax.broadcasted_iota(jnp.int32, (24, LANES), 0) % 8
    lane = lane_iota(1)
    base = first // LANES
    rest = lax.rem(first, LANES)

    def load(b):
        return vel_ref[depth : depth + 1, pl.ds(pl.multiple_of((base + b) * LANES, LANES), LANES)]

    for b in range(blocks):
        cols = slice(b * LANES, (b + 1) * LANES)
        here = load(b)
        other = load(b + 1) if b + 1 < blocks else here
        line = jnp.broadcast_to(jnp.where(lane < rest, other, here), (8, LANES))
        line = pltpu.roll(line, lax.rem(LANES - rest, LANES), 1)
        onehot = (jnp.concatenate([line] * 3, axis=0) == level).astype(F32).astype(BF16)
        out = lax.dot_general(table_ref[...], onehot, (((0,), (0,)), ((), ())), preferred_element_type=F32)
        coef_ref[depth, :, :, :, cols] = out[: taps * 32].reshape(taps, 2, 16, LANES)


def window_of(shot):
    return 0 if shot < 4 else (4 if shot < 12 else 8)


def build_weights(expand_ref, vel_ref, w_ref, depth, first):
    width = expand_ref.shape[2]
    for shot in range(16):
        block = expand_ref[vel_ref[depth, first + shot]]
        lead, rest = divmod(32 * (shot - window_of(shot)), LANES)
        if rest:
            block = pltpu.roll(block, rest, 1)
        block = block.astype(BF16)
        rows = slice(shot * 32, shot * 32 + 32)
        w_ref[depth, rows, :] = jnp.zeros((32, 512), BF16)
        fit = min(width, 512 - lead * LANES)
        w_ref[depth, rows, lead * LANES : lead * LANES + fit] = block[:, :fit]


def place_halo(halo_ref, r_ref, depth, row, delta, blocks, valid):
    lane = lane_iota(16)

    def body(i, carry):
        for c in range(2):
            load = lambda j: halo_ref[depth, i, c, :, j * LANES : (j + 1) * LANES].astype(F32)
            for b in range(blocks):
                moved = jnp.where(valid, shifted(load, b, blocks, delta, lane), 0.0)
                r_ref[depth, row + i, c, :, b * LANES : (b + 1) * LANES] = moved.astype(BF16)
        return carry

    lax.fori_loop(0, 4, body, 0)


def shot_step(w_ref, r_ref, x_ref, live_ref, first, depth, start, stop, blocks):
    lane = lane_iota(16)
    window = window_of(start)
    for lo in range(0, blocks, 3):
        cols = slice(lo * LANES, (lo + 3) * LANES)
        rhs = r_ref[depth, window : window + 16, :, :, cols].reshape(512, 3 * LANES)
        y = jnp.dot(w_ref[depth, start * 32 : stop * 32, :], rhs, preferred_element_type=F32)
        for shot in range(start, stop):
            at = (shot - start) * 32
            for b in range(3):
                keep = keep_mask(lane, lo + b, shot, live_ref[first + shot])
                for c in range(2):
                    part = y[at + c * 16 : at + c * 16 + 16, b * LANES : (b + 1) * LANES].astype(BF16).astype(F32)
                    x_ref[shot, c, :, (lo + b) * LANES : (lo + b + 1) * LANES] = jnp.where(keep, part, 0.0)


def unskew(load, block, shot, lane):
    here = load(block)
    if isinstance(shot, int) and shot == 0:
        return here
    other = load(block + 1)
    return pltpu.roll(jnp.where(lane < shot, other, here), LANES - shot, 1)


def put_image(x_ref, parts_ref, depth, shots, data):
    for shot in shots:
        sums = [jnp.sum(x_ref[shot, 0, :, b * LANES : (b + 1) * LANES], axis=0, keepdims=True) for b in range(data + 1)]
        for b in range(data):
            moved = unskew(lambda i: jnp.broadcast_to(sums[i], (8, LANES)), b, shot, lane_iota())
            parts_ref[depth, b, shot : shot + 1, :] = moved[:1]


def put_out(x_ref, out_ref, shot, data):
    lane = lane_iota(16)
    for c in range(2):
        load = lambda i: x_ref[shot, c, :, i * LANES : (i + 1) * LANES]
        for b in range(data):
            out_ref[c, shot, :, b * LANES : (b + 1) * LANES] = unskew(load, b, shot, lane).astype(BF16)


def kernel(n_src, n_freq, live_ref, vel_smem, vel_ref, taps_ref, wave_ref, image_ref, out_ref,
           x_ref, coef_ref, wide_ref, before_ref, after_ref, w_ref, row_ref, swap_ref, table_ref, expand_ref,
           parts, got, total, full, halo_sems, image_sems):
    src = lax.axis_index("src")
    me = lax.axis_index("freq")
    shots, freqs = wave_ref.shape[1:3]
    data = wave_ref.shape[-1] // LANES
    blocks = wide_ref.shape[-1] // LANES
    depths = wide_ref.shape[0]
    first = src * shots
    ahead, behind = lax.rem(src + 1, n_src), lax.rem(src + n_src - 1, n_src)

    barrier = pltpu.get_barrier_semaphore()
    for peer in (ahead, behind):
        pl.semaphore_signal(barrier, inc=1, device_id={"src": peer}, device_id_type=MESH)
    for step in range(1, n_freq):
        pl.semaphore_signal(barrier, inc=1, device_id={"freq": lax.rem(me + step, n_freq)}, device_id_type=MESH)

    def halo(depth, side):
        return pltpu.make_async_remote_copy(
            src_ref=wide_ref.at[depth, pl.ds(shots if side == 0 else 4, 4)],
            dst_ref=(before_ref if side == 0 else after_ref).at[depth],
            send_sem=halo_sems.at[0, depth, side], recv_sem=halo_sems.at[1, depth, side],
            device_id={"src": ahead if side == 0 else behind}, device_id_type=MESH)

    def scatter(depth, step):
        peer = lax.rem(me + step, n_freq)
        return pltpu.make_async_remote_copy(
            src_ref=parts.at[depth, peer], dst_ref=got.at[depth, step],
            send_sem=image_sems.at[0, depth, step], recv_sem=image_sems.at[1, depth, step],
            device_id={"freq": peer}, device_id_type=MESH)

    def gather(depth, step):
        peer = lax.rem(me + step, n_freq)
        return pltpu.make_async_remote_copy(
            src_ref=total.at[depth], dst_ref=full.at[depth, step],
            send_sem=image_sems.at[2, depth, step], recv_sem=image_sems.at[3, depth, step],
            device_id={"freq": peer}, device_id_type=MESH)

    def send_parts(depth):
        for step in range(1, n_freq):
            scatter(depth, step).start()

    def send_total(depth):
        value = parts[depth, me]
        for step in range(1, n_freq):
            scatter(depth, step).wait()
            value = value + got[depth, step]
        total[depth] = value
        for step in range(1, n_freq):
            gather(depth, step).start()
        image_ref[depth, :, pl.ds(pl.multiple_of(me * LANES, LANES), LANES)] = value

    def take_total(depth):
        for step in range(1, n_freq):
            gather(depth, step).wait()
            owner = lax.rem(me + n_freq - step, n_freq)
            image_ref[depth, :, pl.ds(pl.multiple_of(owner * LANES, LANES), LANES)] = full[depth, step]

    def first_rows(start, stop, jump):
        def body(i, carry):
            shot = i + jump * (i // 4)
            live = live_ref[first + shot]
            load_skewed(wave_ref, x_ref, shot, live, blocks)
            receiver_row(x_ref, coef_ref, 0, wide_ref, shot, shot + 4, live, blocks)
            return carry

        lax.fori_loop(start, stop, body, 0)

    def next_rows(depth, start, stop, jump):
        def body(i, carry):
            shot = i + jump * (i // 4)
            receiver_row(x_ref, coef_ref, depth, wide_ref, shot, shot + 4, live_ref[first + shot], blocks)
            return carry

        lax.fori_loop(start, stop, body, 0)

    def take_halo(depth):
        halo(depth, 0).wait_recv()
        place_halo(before_ref, wide_ref, depth, 0, 16, blocks, src > 0)
        halo(depth, 1).wait_recv()
        place_halo(after_ref, wide_ref, depth, 20, -16, blocks, src < n_src - 1)

    edges = [0, 1, 2, 3, 12, 13, 14, 15]
    inner = list(range(4, 12))
    build_tables(taps_ref, row_ref, swap_ref, table_ref, expand_ref)
    build_coef(table_ref, vel_ref, coef_ref, 0, first, blocks)
    first_rows(0, 8, 8)
    pl.semaphore_wait(barrier, n_freq + 1)
    halo(0, 0).start()
    halo(0, 1).start()
    first_rows(4, 12, 0)
    build_coef(table_ref, vel_ref, coef_ref, 1, first, blocks)
    for depth in range(depths):
        build_weights(expand_ref, vel_smem, w_ref, depth, first)
    shot_step(w_ref, wide_ref, x_ref, live_ref, first, 0, 4, 12, blocks)
    next_rows(1, 4, 12, 0)
    put_image(x_ref, parts, 0, inner, data)
    take_halo(0)
    shot_step(w_ref, wide_ref, x_ref, live_ref, first, 0, 0, 4, blocks)
    shot_step(w_ref, wide_ref, x_ref, live_ref, first, 0, 12, 16, blocks)
    next_rows(1, 0, 8, 8)
    halo(1, 0).start()
    halo(1, 1).start()
    put_image(x_ref, parts, 0, edges, data)
    send_parts(0)

    def out_rows(start, stop, jump):
        def body(i, carry):
            put_out(x_ref, out_ref, i + jump * (i // 4), data)
            return carry

        lax.fori_loop(start, stop, body, 0)

    shot_step(w_ref, wide_ref, x_ref, live_ref, first, 1, 4, 12, blocks)
    put_image(x_ref, parts, 1, inner, data)
    out_rows(4, 12, 0)
    send_total(0)
    take_halo(1)
    shot_step(w_ref, wide_ref, x_ref, live_ref, first, 1, 0, 4, blocks)
    shot_step(w_ref, wide_ref, x_ref, live_ref, first, 1, 12, 16, blocks)
    put_image(x_ref, parts, 1, edges, data)
    send_parts(1)
    out_rows(0, 8, 8)
    take_total(0)
    send_total(1)
    for depth in range(depths):
        for side in range(2):
            halo(depth, side).wait_send()
    take_total(1)


def local(wave, live, vel_index, taps):
    shots, freqs, width = wave.shape[1:]
    levels, count = taps.shape[1], taps.shape[3]
    depths = vel_index.shape[0]
    wide = width + LANES
    n_src = lax.axis_size("src")
    n_freq = lax.axis_size("freq")
    smem = pl.BlockSpec(memory_space=pltpu.SMEM)
    vmem = pl.BlockSpec(memory_space=pltpu.VMEM)
    halo_buf = pltpu.VMEM((depths, 4, 2, freqs, wide), BF16)
    piece = pltpu.VMEM((depths, n_freq, shots, LANES), F32)
    tap_row = pltpu.VMEM((levels, 384), F32)
    return pl.pallas_call(
        functools.partial(kernel, n_src, n_freq),
        out_shape=(jax.ShapeDtypeStruct((depths, shots, width), F32), jax.ShapeDtypeStruct(wave.shape, BF16)),
        in_specs=[smem, smem, vmem, vmem, vmem], out_specs=(vmem, vmem),
        scratch_shapes=[
            pltpu.VMEM((shots, 2, freqs, wide), F32),
            pltpu.VMEM((depths, count, 2, freqs, wide), F32),
            pltpu.VMEM((depths, shots + 8, 2, freqs, wide), BF16),
            halo_buf, halo_buf,
            pltpu.VMEM((depths, 512, 512), BF16),
            tap_row, tap_row,
            pltpu.VMEM((3 * levels, 384), BF16),
            pltpu.VMEM((levels, 2 * freqs, 384), F32),
            piece, piece, pltpu.VMEM((depths, shots, LANES), F32), piece,
            pltpu.SemaphoreType.DMA((2, depths, 2)),
            pltpu.SemaphoreType.DMA((4, depths, n_freq)),
        ],
        compiler_params=pltpu.CompilerParams(collective_id=0, has_side_effects=True, vmem_limit_bytes=60 * 1024 * 1024),
    )(live, vel_index, vel_index, jnp.transpose(taps, (0, 3, 1, 2)), wave)


def solution(mesh):
    placed = (P(None, "src", "freq", None), P(), P(), P(None, None, "freq", None))
    return jax.shard_map(
        local, mesh=mesh, in_specs=placed,
        out_specs=(P(None, "src", None), P(None, "src", "freq", None)), check_vma=False,
    )
```

time: 87.7 us -> 50 us (0.57)
  the two profiles are of different devices: /device:TPU:6 before, /device:TPU:24 now
where the time goes in v1:
time: 50 us; the launch traced here: 49.9 us
  Pallas kernels  45.3 us (91%)
  local copies, waits for them, and re-layouts  3.87 us (8%)
  between operations  0.64 us (1%)
    pallas_call x1, Pallas kernels, local(): pl.pallas_call(functools.partial(kernel, n_src, n_freq), out_shape=(jax.S...  45.3 us
    unnamed x2, local copies, waits for them, and re-layouts  3.87 us

profile of v1, /device:TPU:24, one launch (start us, length us, event | category | flops | bytes accessed | tf_op | source)
XLA Modules:
  0.0 49.9 jit_solution(10568001490580210764)
XLA Ops:
  0.6 45.3 %shard_map.59 = (f32[2,16,1024]{2,1,0:T(8,128)}, bf16[2,16,16,1024]{3,2,1,0:T(8,128)(2,1)}) custom-call(s32[512]{0:T(512)} %live_ref.1, s32[2,1536]{1,0:T(2,128)} %vel_ref.1, s32[2,1536]{1,0:T(2,128)} %vel_ref.1, f32[2,9,8,16]{3,2,1,0:T(8,128)} %bitcast.1, bf16[2,16,16,1024]{3,2,1,0:T(8,128)(2,1)} %wave_ref.1), custom_call_target="tpu_custom_call" | custom-call | tf_op jit(solution)/shard_map/pallas_call | solution.py:347
  46.0 1.6 %copy.8 = f32[2,16,1024]{2,1,0:T(8,128)} copy(f32[2,16,1024]{2,1,0:T(8,128)} %get-tuple-element.4) | data formatting | bytes 262144
  47.5 2.3 %copy.9 = bf16[2,16,16,1024]{3,2,1,0:T(8,128)(2,1)} copy(bf16[2,16,16,1024]{3,2,1,0:T(8,128)(2,1)} %get-tuple-element.5) | data formatting | bytes 2097152

commit v2 on v1

--- a/solution.py
+++ b/solution.py
@@ -146,18 +146,13 @@
         w_ref[depth, rows, lead * LANES : lead * LANES + fit] = block[:, :fit]
 
 
-def place_halo(halo_ref, r_ref, depth, row, delta, blocks, valid):
+def place_halo(halo_ref, r_ref, depth, i, row, delta, blocks, valid):
     lane = lane_iota(16)
-
-    def body(i, carry):
-        for c in range(2):
-            load = lambda j: halo_ref[depth, i, c, :, j * LANES : (j + 1) * LANES].astype(F32)
-            for b in range(blocks):
-                moved = jnp.where(valid, shifted(load, b, blocks, delta, lane), 0.0)
-                r_ref[depth, row + i, c, :, b * LANES : (b + 1) * LANES] = moved.astype(BF16)
-        return carry
-
-    lax.fori_loop(0, 4, body, 0)
+    for c in range(2):
+        load = lambda j: halo_ref[depth, i, c, :, j * LANES : (j + 1) * LANES].astype(F32)
+        for b in range(blocks):
+            moved = jnp.where(valid, shifted(load, b, blocks, delta, lane), 0.0)
+            r_ref[depth, row, c, :, b * LANES : (b + 1) * LANES] = moved.astype(BF16)
 
 
 def shot_step(w_ref, r_ref, x_ref, live_ref, first, depth, start, stop, blocks):
@@ -200,9 +195,9 @@
             out_ref[c, shot, :, b * LANES : (b + 1) * LANES] = unskew(load, b, shot, lane).astype(BF16)
 
 
-def kernel(n_src, n_freq, live_ref, vel_smem, vel_ref, taps_ref, wave_ref, image_ref, out_ref,
+def kernel(n_src, n_freq, live_ref, vel_smem, vel_ref, taps_ref, wave_hbm, image_ref, out_hbm, wave_ref, out_ref,
            x_ref, coef_ref, wide_ref, before_ref, after_ref, w_ref, row_ref, swap_ref, table_ref, expand_ref,
-           parts, got, total, full, halo_sems, image_sems):
+           parts, got, total, full, halo_sems, image_sems, copy_sems):
     src = lax.axis_index("src")
     me = lax.axis_index("freq")
     shots, freqs = wave_ref.shape[1:3]
@@ -218,11 +213,20 @@
     for step in range(1, n_freq):
         pl.semaphore_signal(barrier, inc=1, device_id={"freq": lax.rem(me + step, n_freq)}, device_id_type=MESH)
 
-    def halo(depth, side):
+    def wave_in(side):
+        return pltpu.make_async_copy(wave_hbm.at[side], wave_ref.at[side], copy_sems.at[0, side])
+
+    def wave_back(shot):
+        return pltpu.make_async_copy(out_ref.at[:, shot], out_hbm.at[:, shot], copy_sems.at[1, shot])
+
+    for side in range(2):
+        wave_in(side).start()
+
+    def halo(depth, side, h):
         return pltpu.make_async_remote_copy(
-            src_ref=wide_ref.at[depth, pl.ds(shots if side == 0 else 4, 4)],
-            dst_ref=(before_ref if side == 0 else after_ref).at[depth],
-            send_sem=halo_sems.at[0, depth, side], recv_sem=halo_sems.at[1, depth, side],
+            src_ref=wide_ref.at[depth, shots + 3 - h if side == 0 else 4 + h],
+            dst_ref=before_ref.at[depth, 3 - h] if side == 0 else after_ref.at[depth, h],
+            send_sem=halo_sems.at[0, depth, side, h], recv_sem=halo_sems.at[1, depth, side, h],
             device_id={"src": ahead if side == 0 else behind}, device_id_type=MESH)
 
     def scatter(depth, step):
@@ -259,57 +263,68 @@
             owner = lax.rem(me + n_freq - step, n_freq)
             image_ref[depth, :, pl.ds(pl.multiple_of(owner * LANES, LANES), LANES)] = full[depth, step]
 
-    def first_rows(start, stop, jump):
-        def body(i, carry):
-            shot = i + jump * (i // 4)
-            live = live_ref[first + shot]
-            load_skewed(wave_ref, x_ref, shot, live, blocks)
-            receiver_row(x_ref, coef_ref, 0, wide_ref, shot, shot + 4, live, blocks)
+    def first_row(shot):
+        live = live_ref[first + shot]
+        load_skewed(wave_ref, x_ref, shot, live, blocks)
+        receiver_row(x_ref, coef_ref, 0, wide_ref, shot, shot + 4, live, blocks)
+
+    def next_row(shot):
+        receiver_row(x_ref, coef_ref, 1, wide_ref, shot, shot + 4, live_ref[first + shot], blocks)
+
+    def inner_rows(step):
+        def body(shot, carry):
+            step(shot)
             return carry
 
-        lax.fori_loop(start, stop, body, 0)
-
-    def next_rows(depth, start, stop, jump):
-        def body(i, carry):
-            shot = i + jump * (i // 4)
-            receiver_row(x_ref, coef_ref, depth, wide_ref, shot, shot + 4, live_ref[first + shot], blocks)
+        lax.fori_loop(4, 12, body, 0)
+
+    def edge_rows(step, depth, start):
+        def body(h, carry):
+            step(h)
+            halo(depth, 1, h).start()
+            step(15 - h)
+            halo(depth, 0, h).start()
             return carry
 
-        lax.fori_loop(start, stop, body, 0)
+        lax.fori_loop(start, 4, body, 0)
 
     def take_halo(depth):
-        halo(depth, 0).wait_recv()
-        place_halo(before_ref, wide_ref, depth, 0, 16, blocks, src > 0)
-        halo(depth, 1).wait_recv()
-        place_halo(after_ref, wide_ref, depth, 20, -16, blocks, src < n_src - 1)
+        def body(h, carry):
+            halo(depth, 1, h).wait_recv()
+            place_halo(after_ref, wide_ref, depth, h, 20 + h, -16, blocks, src < n_src - 1)
+            halo(depth, 0, h).wait_recv()
+            place_halo(before_ref, wide_ref, depth, 3 - h, 3 - h, 16, blocks, src > 0)
+            return carry
+
+        lax.fori_loop(0, 4, body, 0)
 
     edges = [0, 1, 2, 3, 12, 13, 14, 15]
     inner = list(range(4, 12))
     build_tables(taps_ref, row_ref, swap_ref, table_ref, expand_ref)
     build_coef(table_ref, vel_ref, coef_ref, 0, first, blocks)
-    first_rows(0, 8, 8)
+    for side in range(2):
+        wave_in(side).wait()
     pl.semaphore_wait(barrier, n_freq + 1)
-    halo(0, 0).start()
-    halo(0, 1).start()
-    first_rows(4, 12, 0)
+    edge_rows(first_row, 0, 0)
+    inner_rows(first_row)
     build_coef(table_ref, vel_ref, coef_ref, 1, first, blocks)
     for depth in range(depths):
         build_weights(expand_ref, vel_smem, w_ref, depth, first)
     shot_step(w_ref, wide_ref, x_ref, live_ref, first, 0, 4, 12, blocks)
-    next_rows(1, 4, 12, 0)
+    inner_rows(next_row)
     put_image(x_ref, parts, 0, inner, data)
     take_halo(0)
     shot_step(w_ref, wide_ref, x_ref, live_ref, first, 0, 0, 4, blocks)
     shot_step(w_ref, wide_ref, x_ref, live_ref, first, 0, 12, 16, blocks)
-    next_rows(1, 0, 8, 8)
-    halo(1, 0).start()
-    halo(1, 1).start()
+    edge_rows(next_row, 1, 0)
     put_image(x_ref, parts, 0, edges, data)
     send_parts(0)
 
     def out_rows(start, stop, jump):
         def body(i, carry):
-            put_out(x_ref, out_ref, i + jump * (i // 4), data)
+            shot = i + jump * (i // 4)
+            put_out(x_ref, out_ref, shot, data)
+            wave_back(shot).start()
             return carry
 
         lax.fori_loop(start, stop, body, 0)
@@ -328,7 +343,10 @@
     send_total(1)
     for depth in range(depths):
         for side in range(2):
-            halo(depth, side).wait_send()
+            for h in range(4):
+                halo(depth, side, h).wait_send()
+    for shot in range(shots):
+        wave_back(shot).wait()
     take_total(1)
 
 
@@ -341,14 +359,17 @@
     n_freq = lax.axis_size("freq")
     smem = pl.BlockSpec(memory_space=pltpu.SMEM)
     vmem = pl.BlockSpec(memory_space=pltpu.VMEM)
+    away = pl.BlockSpec(memory_space=pl.ANY)
     halo_buf = pltpu.VMEM((depths, 4, 2, freqs, wide), BF16)
     piece = pltpu.VMEM((depths, n_freq, shots, LANES), F32)
     tap_row = pltpu.VMEM((levels, 384), F32)
     return pl.pallas_call(
         functools.partial(kernel, n_src, n_freq),
         out_shape=(jax.ShapeDtypeStruct((depths, shots, width), F32), jax.ShapeDtypeStruct(wave.shape, BF16)),
-        in_specs=[smem, smem, vmem, vmem, vmem], out_specs=(vmem, vmem),
+        in_specs=[smem, smem, vmem, vmem, away], out_specs=(vmem, away),
         scratch_shapes=[
+            pltpu.VMEM(wave.shape, BF16),
+            pltpu.VMEM(wave.shape, BF16),
             pltpu.VMEM((shots, 2, freqs, wide), F32),
             pltpu.VMEM((depths, count, 2, freqs, wide), F32),
             pltpu.VMEM((depths, shots + 8, 2, freqs, wide), BF16),
@@ -358,8 +379,9 @@
             pltpu.VMEM((3 * levels, 384), BF16),
             pltpu.VMEM((levels, 2 * freqs, 384), F32),
             piece, piece, pltpu.VMEM((depths, shots, LANES), F32), piece,
-            pltpu.SemaphoreType.DMA((2, depths, 2)),
+            pltpu.SemaphoreType.DMA((2, depths, 2, 4)),
             pltpu.SemaphoreType.DMA((4, depths, n_freq)),
+            pltpu.SemaphoreType.DMA((2, shots)),
         ],
         compiler_params=pltpu.CompilerParams(collective_id=0, has_side_effects=True, vmem_limit_bytes=60 * 1024 * 1024),
     )(live, vel_index, vel_index, jnp.transpose(taps, (0, 3, 1, 2)), wave)

time: 50 us -> 48.4 us (0.968)
  the two profiles are of different devices: /device:TPU:24 before, /device:TPU:6 now
where the time goes in v2:
time: 48.4 us; the launch traced here: 47.5 us
  Pallas kernels  43 us (89%)
  local copies, waits for them, and re-layouts  3.87 us (8%)
  between operations  0.64 us (1%)
    pallas_call x1, Pallas kernels, local(): pl.pallas_call(functools.partial(kernel, n_src, n_freq), out_shape=(jax.S...  43 us
    unnamed x2, local copies, waits for them, and re-layouts  3.87 us

profile of v2, /device:TPU:6, one launch (start us, length us, event | category | flops | bytes accessed | tf_op | source)
XLA Modules:
  0.0 47.5 jit_solution(7848328741759832850)
XLA Ops:
  0.6 43.0 %shard_map.59 = (f32[2,16,1024]{2,1,0:T(8,128)}, bf16[2,16,16,1024]{3,2,1,0:T(8,128)(2,1)}) custom-call(s32[512]{0:T(512)} %live_ref.1, s32[2,1536]{1,0:T(2,128)} %vel_ref.1, s32[2,1536]{1,0:T(2,128)} %vel_ref.1, f32[2,9,8,16]{3,2,1,0:T(8,128)} %bitcast.1, bf16[2,16,16,1024]{3,2,1,0:T(8,128)(2,1)} %wave_hbm.1), custom_call_target="tpu_custom_call" | custom-call | tf_op jit(solution)/shard_map/pallas_call | solution.py:366
  43.6 1.6 %copy.8 = f32[2,16,1024]{2,1,0:T(8,128)} copy(f32[2,16,1024]{2,1,0:T(8,128)} %get-tuple-element.4) | data formatting | bytes 262144
  45.2 2.3 %copy.9 = bf16[2,16,16,1024]{3,2,1,0:T(8,128)(2,1)} copy(bf16[2,16,16,1024]{3,2,1,0:T(8,128)(2,1)} %get-tuple-element.5) | data formatting | bytes 2097152
